TPU v7x, 512 devices: a whole 4x4x16 slice. The times are simulated.
512 devices in a mesh: blk: 16 (over y, x_hi, core), group: 32 (over x_lo, z).
Axes of the slice: x: 4 (x_hi: 2, x_lo: 2; x = x_hi * 2 + x_lo), y: 4, z: 16, core: 2. Of those that a mesh axis runs over, the one named last changes fastest.
Arguments:
- student_features: bfloat16 [65536, 768], P(('blk', 'group')), may hold values from -8 to 8
- teacher_image: bfloat16 [65536, 1152], P(('blk', 'group')), may hold values from -8 to 8
- text_embeds: bfloat16 [65536, 1152], P(('blk', 'group')), may hold values from -8 to 8
- pair_ids: int32 [65536], replicated, may hold values from 0 to 8191
- head_weights: bfloat16 [1152, 768], replicated, may hold values from -1 to 1
- moment_first: float32 [1152, 768], P('group'), may hold values from -4 to 4
- moment_second: float32 [1152, 768], P('group'), may hold values from 0.01 to 0.3
Outputs:
- row_loss: float32 [65536], P(('blk', 'group'))
- new_first: float32 [1152, 768], P('group')
- new_second: float32 [1152, 768], P('group')
- new_weights: bfloat16 [1152, 768], replicated
All inputs are finite; a program needn't handle non-finite values.
Results may differ from a plain program's by a relative error of at most 0.0025.
The roundings to bfloat16 on the way count: a program that leaves them out, or rounds other values in their place, can miss the bound.
Values may be sent and summed in bfloat16 or wider, within the bound.
No kernel may reach another device: no remote copies, remote signals or barrier semaphores. Data moves between devices by JAX's collectives and lax.ppermute only.
A program may use at most 64 MiB of HBM per device.

v0:
```python
import functools

import jax
import jax.numpy as jnp
import numpy as np
from jax import lax
from jax.experimental import pallas as pl
from jax.experimental.pallas import tpu as pltpu
from jax.sharding import PartitionSpec as P


student_scale = 20.0
student_bias = -1.0
teacher_scale = 25.0
teacher_bias = -1.5
label_mix = 0.5
norm_eps = 1e-06
beta_one = 0.9
beta_two = 0.95
learn_rate = 0.01
weight_decay = 0.0001
adam_eps = 1e-08
adam_step = 100.0

AXES = ("blk", "group")


def device(X, y, core, z):
    return (y * 4 + X % 2 * 2 + core) * 32 + X // 2 * 16 + z


def x_line(y, core, z):
    return [device(X, y, core, z) for X in range(4)]


def y_line(X, core, z):
    return [device(X, y, core, z) for y in range(4)]


def lines(along_x):
    groups = []
    for core in range(2):
        line = x_line if (core == 0) == along_x else y_line
        groups += [line(i, core, z) for z in range(16) for i in range(4)]
    return groups


FIRST = lines(True)
SECOND = lines(False)
PLANE = [
    [device(X, y, core, z) for X in range(4) for y in range(4)]
    for core in range(2)
    for z in range(16)
]
COLUMN = [
    [device(X, y, core, z) for z in range(16)]
    for X in range(4)
    for y in range(4)
    for core in range(2)
]
TWIN = [(i, i ^ 32) for i in range(512)]


def hop(step):
    pairs = []
    for i in range(512):
        blk, group = divmod(i, 32)
        y, xh, core = blk // 4, blk // 2 % 2, blk % 2
        xl, z = divmod(group, 16)
        x = xh * 2 + xl
        if core == 0:
            y = (y + step) % 4
        else:
            x = (x + step) % 4
        pairs.append((i, device(x % 2 * 2 + x // 2, y, core, z)))
    return pairs


FORTH = hop(1)
BACK = hop(-1)


def exchange(pieces, groups):
    return lax.all_to_all(pieces, AXES, 0, 0, axis_index_groups=groups, tiled=True)


def share(block, groups):
    return exchange(jnp.broadcast_to(block[None], (len(groups[0]), *block.shape)), groups)


def from_twin(shard):
    return lax.ppermute(shard, AXES, TWIN)


def unit_rows(values):
    values = values.astype(jnp.float32)
    return values * lax.rsqrt(jnp.sum(values * values, axis=-1, keepdims=True) + norm_eps)


def head_kernel(texts_ref, features_ref, teacher_ref, out_ref, unit_ref, texts, teacher, packed, unit, sems):
    width = texts_ref.shape[1]
    take_texts = pltpu.make_async_copy(texts_ref, texts, sems.at[0])
    take_features = pltpu.make_async_copy(features_ref, packed.at[:, width:], sems.at[1])
    take_teacher = pltpu.make_async_copy(teacher_ref, teacher, sems.at[2])
    take_texts.start()
    take_features.start()
    take_teacher.start()
    take_texts.wait()
    packed[:, :width] = unit_rows(texts[...]).astype(jnp.bfloat16)
    take_features.wait()
    puts = [
        pltpu.make_async_copy(packed, out_ref.at[i], sems.at[3 + i])
        for i in range(out_ref.shape[0])
    ]
    for put in puts:
        put.start()
    take_teacher.wait()
    unit[...] = unit_rows(teacher[...]).astype(jnp.bfloat16)
    put_unit = pltpu.make_async_copy(unit, unit_ref, sems.at[3 + len(puts)])
    put_unit.start()
    for put in puts:
        put.wait()
    put_unit.wait()


def head(texts, features, teacher, count):
    rows, width = texts.shape[0], texts.shape[1] + features.shape[1]
    return pl.pallas_call(
        head_kernel,
        out_shape=(
            jax.ShapeDtypeStruct((count, rows, width), jnp.bfloat16),
            jax.ShapeDtypeStruct(teacher.shape, jnp.bfloat16),
        ),
        in_specs=[pl.BlockSpec(memory_space=pltpu.HBM)] * 3,
        out_specs=(pl.BlockSpec(memory_space=pltpu.HBM),) * 2,
        scratch_shapes=[
            pltpu.VMEM(texts.shape, jnp.bfloat16),
            pltpu.VMEM(teacher.shape, jnp.bfloat16),
            pltpu.VMEM((rows, width), jnp.bfloat16),
            pltpu.VMEM(teacher.shape, jnp.bfloat16),
            pltpu.SemaphoreType.DMA((4 + count,)),
        ],
        compiler_params=pltpu.CompilerParams(vmem_limit_bytes=60 << 20),
        cost_estimate=pl.CostEstimate(
            flops=8 * texts.size, bytes_accessed=2 * (count + 2) * rows * width, transcendentals=0
        ),
    )(texts, features, teacher)


def column_kernel(core_ref, parts_ref, others_ref, keep_ref, send_ref):
    def put(keep, send):
        keep_ref[...] = jnp.sum(parts_ref[:, :, keep], axis=0)
        send_ref[:80, :] = jnp.sum(parts_ref[:, :, send], axis=0)

    left, right = slice(0, 384), slice(384, 768)

    @pl.when(core_ref[0] == 0)
    def _():
        put(left, right)

    @pl.when(core_ref[0] != 0)
    def _():
        put(right, left)

    send_ref[80:, :] = others_ref[...]


def column_sums(core, parts, others):
    whole = pl.BlockSpec(memory_space=pltpu.VMEM)
    return pl.pallas_call(
        column_kernel,
        out_shape=(
            jax.ShapeDtypeStruct((80, 384), jnp.float32),
            jax.ShapeDtypeStruct((88, 384), jnp.float32),
        ),
        in_specs=[pl.BlockSpec(memory_space=pltpu.SMEM), whole, whole],
        out_specs=(whole, whole),
        compiler_params=pltpu.CompilerParams(vmem_limit_bytes=12 << 20),
        cost_estimate=pl.CostEstimate(flops=4 * 80 * 768, bytes_accessed=2 << 20, transcendentals=0),
    )(core.reshape(1), parts, others)


def select_kernel(xl_ref, rows_ref, plane_ref, out_ref):
    def picked(count, which, part):
        rows = lax.broadcasted_iota(jnp.int32, (count, rows_ref.shape[1]), 0)
        chosen = (rows == rows_ref[which : which + 1, :]).astype(jnp.bfloat16)
        return [
            jnp.dot(chosen, values, preferred_element_type=jnp.float32).astype(jnp.bfloat16)
            for values in part
        ]

    low, high = picked(576, 0, (plane_ref[0], plane_ref[1]))
    out_ref[:576, :] = low
    out_ref[576:1152, :] = high
    (out_ref[1152:, :],) = picked(144, 1, (plane_ref[xl_ref[0]],))


def selected(xl, plane):
    whole = pl.BlockSpec(memory_space=pltpu.VMEM)
    return pl.pallas_call(
        select_kernel,
        out_shape=jax.ShapeDtypeStruct((1296, 384), jnp.bfloat16),
        in_specs=[pl.BlockSpec(memory_space=pltpu.SMEM), whole, whole],
        out_specs=whole,
        compiler_params=pltpu.CompilerParams(vmem_limit_bytes=12 << 20),
        cost_estimate=pl.CostEstimate(
            flops=2 * 1296 * 768 * 384, bytes_accessed=2 << 20, transcendentals=0
        ),
    )(xl.reshape(1), jnp.asarray(place_rows()), plane)


def last_kernel(core_ref, half_ref, twin_ref, first_ref, second_ref, *outs):
    weights_ref, new_first_ref, new_second_ref, sems = outs

    def put(left, right):
        copies = [
            pltpu.make_async_copy(
                ref.at[:1152, :], weights_ref.at[:, side * 384 : side * 384 + 384], sems.at[side]
            )
            for side, ref in enumerate((left, right))
        ]
        for copy in copies:
            copy.start()
        for side, ref in enumerate((left, right)):
            columns = slice(side * 384, side * 384 + 384)
            high, middle, low = (
                ref[1152 + i * 48 : 1200 + i * 48, :].astype(jnp.float32) for i in range(3)
            )
            grad = ((high + middle) + low)[:36]
            new_first_ref[:, columns] = beta_one * first_ref[:, columns] + (1.0 - beta_one) * grad
            new_second_ref[:, columns] = (
                beta_two * second_ref[:, columns] + (1.0 - beta_two) * grad * grad
            )
        for copy in copies:
            copy.wait()

    @pl.when(core_ref[0] == 0)
    def _():
        put(half_ref, twin_ref)

    @pl.when(core_ref[0] != 0)
    def _():
        put(twin_ref, half_ref)


def last_outputs(core, half, twin_half, moment_first, moment_second):
    whole = pl.BlockSpec(memory_space=pltpu.VMEM)
    moment = jax.ShapeDtypeStruct(moment_first.shape, jnp.float32)
    return pl.pallas_call(
        last_kernel,
        out_shape=(jax.ShapeDtypeStruct((1152, 768), jnp.bfloat16), moment, moment),
        in_specs=[pl.BlockSpec(memory_space=pltpu.SMEM)] + [whole] * 4,
        out_specs=(pl.BlockSpec(memory_space=pltpu.HBM), whole, whole),
        scratch_shapes=[pltpu.SemaphoreType.DMA((2,))],
        compiler_params=pltpu.CompilerParams(vmem_limit_bytes=12 << 20),
        cost_estimate=pl.CostEstimate(flops=0, bytes_accessed=6 << 20, transcendentals=0),
    )(core.reshape(1), half, twin_half, moment_first, moment_second)


def pair_terms(student_rows, teacher_rows, left_ids, text_rows, right_ids):
    dims = (((1,), (1,)), ((), ()))
    student_logit = (
        student_scale
        * lax.dot_general(student_rows, text_rows, dims, preferred_element_type=jnp.float32)
        + student_bias
    )
    teacher_logit = (
        teacher_scale
        * lax.dot_general(teacher_rows, text_rows, dims, preferred_element_type=jnp.float32)
        + teacher_bias
    )
    labels = (left_ids == right_ids).astype(jnp.float32)
    target = (1.0 - label_mix) * labels + label_mix * jax.nn.sigmoid(teacher_logit)
    tail = jnp.exp(-jnp.abs(student_logit))
    softplus = jnp.maximum(student_logit, 0.0) + jnp.log1p(tail)
    chance = jnp.where(student_logit >= 0.0, 1.0, tail) / (1.0 + tail)
    losses = jnp.sum(softplus - target * student_logit, axis=1, keepdims=True)
    return losses, (chance - target).astype(jnp.bfloat16)


def pair_kernel(places, carried, last, *refs):
    student_ref, own_teacher_ref, twin_teacher_ref, left_ref, ids_ref = refs[:5]
    chunks, rest = refs[5 : 5 + len(places)], refs[5 + len(places) :]
    pulled_ref, losses_ref = rest[-2:]
    if last:
        own_ref, twin_ref, losses_ref, others_ref, pulled_ref = rest[-5:]
    if carried:
        pulled_ref[...] = rest[0][...]
        total = rest[1][...]
    else:
        pulled_ref[...] = jnp.zeros_like(pulled_ref)
        total = jnp.zeros(losses_ref.shape, jnp.float32)
    teacher = jnp.concatenate([own_teacher_ref[...], twin_teacher_ref[...]], axis=0)
    left_ids = jnp.concatenate(
        [jnp.transpose(jnp.broadcast_to(left_ref[i : i + 1, :], (128, 128))) for i in range(2)], axis=0
    )[:, :1]
    for place, chunk_ref in zip(places, chunks):
        texts = chunk_ref[...]
        losses, coeff = pair_terms(
            student_ref[...], teacher, left_ids, texts, ids_ref[place : place + 1, :]
        )
        total += losses
        pulled_ref[...] += jnp.dot(coeff, texts, preferred_element_type=jnp.float32)
    if not last:
        losses_ref[...] = total
        return
    own_ref[...] = pulled_ref[:128]
    twin_ref[...] = pulled_ref[128:]
    lanes = [
        jnp.transpose(jnp.broadcast_to(total[i * 128 : i * 128 + 128], (128, 128)))[:1]
        for i in range(2)
    ]
    losses_ref[...] = lanes[0]
    others_ref[...] = jnp.zeros_like(others_ref)
    others_ref[:1, :128] = lanes[1]


def pair_sums(student_rows, own_teacher, twin_teacher, left_ids, text_ids, chunks, carried=(), last=False):
    rows, width = student_rows.shape
    texts, places = zip(*chunks)
    count = sum(chunk.shape[0] for chunk in texts)
    operands = (student_rows, own_teacher, twin_teacher, left_ids, text_ids, *texts, *carried)
    whole = pl.BlockSpec(memory_space=pltpu.VMEM)
    parts = 1 + last
    shapes = [(rows // parts, width)] * parts + ([(1, 128), (8, 384)] if last else [(rows, 1)])
    return pl.pallas_call(
        functools.partial(pair_kernel, places, bool(carried), last),
        out_shape=[jax.ShapeDtypeStruct(shape, jnp.float32) for shape in shapes],
        in_specs=[whole] * len(operands),
        out_specs=[whole] * len(shapes),
        scratch_shapes=[pltpu.VMEM((rows, width), jnp.float32)] * last,
        compiler_params=pltpu.CompilerParams(vmem_limit_bytes=20 << 20),
        cost_estimate=pl.CostEstimate(
            flops=6 * rows * count * width,
            bytes_accessed=2 * count * width,
            transcendentals=4 * rows * count,
        ),
    )(*operands)


def row_order(core):
    place = lax.iota(jnp.int32, 1280)
    first, second = place // 320, place // 80 % 4
    X = jnp.where(core == 0, first, second)
    y = jnp.where(core == 0, second, first)
    row = (X % 2 * 4 + y) * 5 + place % 5
    return jnp.where(row < 36, X // 2 * 576 + place // 5 % 16 * 36 + row, -1)


def place_rows():
    chip, row = np.arange(768) // 96, np.arange(768) % 96
    q = chip * 5 + row % 5
    weights = np.where((row < 80) & (q < 36), row // 5 * 36 + q, -1)
    grads = np.where((row >= 80) & (row < 95), (row - 80) // 5 * 48 + q, -1)
    return np.stack([weights, grads]).astype(np.int32)


def one_hot(index, width):
    return (index[:, None] == lax.iota(jnp.int32, width)[None, :]).astype(jnp.bfloat16)


def rounded(values):
    return lax.reduce_precision(values, 8, 7)


def per_device(
    student_features,
    teacher_image,
    text_embeds,
    pair_ids,
    head_weights,
    moment_first,
    moment_second,
):
    rows = student_features.shape[0]
    blk_index = lax.axis_index("blk")
    group_index = lax.axis_index("group")
    y, xh, core = blk_index // 4, blk_index // 2 % 2, blk_index % 2
    xl, z = group_index // 16, group_index % 16

    copies, unit_teacher = head(text_embeds, student_features, teacher_image, 4)
    copies, twin_features = lax.optimization_barrier((copies, student_features))
    near = exchange(copies, FIRST)

    far_features, far_teacher = from_twin(twin_features), from_twin(unit_teacher)
    both_features = jnp.concatenate([student_features, far_features], axis=0)
    projected = lax.dot_general(
        both_features,
        head_weights,
        (((1,), (1,)), ((), ())),
        preferred_element_type=jnp.float32,
    )
    inverse = lax.rsqrt(jnp.sum(projected * projected, axis=-1, keepdims=True) + norm_eps)
    student = projected * inverse
    student_b = student.astype(jnp.bfloat16)

    ids_grid = pair_ids.reshape(4, 2, 2, 2, 16, rows)
    ids_plane = lax.dynamic_index_in_dim(ids_grid, z, 4, keepdims=False)
    ids_core = lax.dynamic_index_in_dim(ids_plane, core, 2, keepdims=False)
    ids_yx = ids_core.transpose(0, 2, 1, 3).reshape(4, 4, rows)
    ids_xy = ids_core.transpose(1, 2, 0, 3).reshape(4, 4, rows)
    text_ids = jnp.where(core == 0, ids_yx, ids_xy)
    text_ids = jnp.concatenate([text_ids, text_ids[:3]], axis=0)
    text_ids = lax.dynamic_slice_in_dim(text_ids, jnp.where(core == 0, y, xh * 2 + xl), 4, 0)
    text_ids = text_ids.reshape(8, 2 * rows)
    ids_rows = pair_ids.reshape(512, rows)
    left_ids = jnp.stack(
        [
            lax.dynamic_index_in_dim(ids_rows, blk_index * 32 + group_index, 0, keepdims=False),
            lax.dynamic_index_in_dim(ids_rows, (blk_index ^ 1) * 32 + group_index, 0, keepdims=False),
        ]
    )

    def piece(values, start):
        group_rows = lax.dynamic_slice_in_dim(values, start, 36, 0)
        padded = jnp.pad(group_rows, ((0, 4), (0, 0)))
        return lax.dynamic_slice(padded, ((xh * 4 + y) * 5, core * 384), (5, 384))

    weight_rows = piece(head_weights, group_index * 36)
    near, weight_rows, *images = lax.optimization_barrier(
        (near, weight_rows, student_b, unit_teacher, far_teacher, left_ids, text_ids)
    )

    top = near[:2, :, :1152].reshape(2 * rows, 1152)
    bottom = near[2:, :, :1152].reshape(2 * rows, 1152)
    before_top = lax.ppermute(top, AXES, FORTH)
    after_bottom = lax.ppermute(bottom, AXES, BACK)
    before_bottom = lax.ppermute(bottom, AXES, FORTH)
    after_top = lax.ppermute(top, AXES, BACK)
    far_top = lax.ppermute(before_top, AXES, FORTH)
    far_bottom = lax.ppermute(after_bottom, AXES, BACK)
    sums = pair_sums(*images, [(top, 0), (bottom, 1)])
    near_chunks = [(before_top, 6), (after_bottom, 3), (before_bottom, 7), (after_top, 2)]
    sums = pair_sums(*images, near_chunks, sums)
    features = near[:, :, 1152:]
    features, sums = lax.optimization_barrier((features, sums))
    far_chunks = [(far_top, 4), (far_bottom, 5)]
    pulled, twin_pulled, losses, other_losses = pair_sums(*images, far_chunks, sums, last=True)

    pulled = pulled + from_twin(twin_pulled)
    student, inverse = student[:rows], inverse[:rows]
    grad_student = student_scale / rows * pulled
    grad_projected = (
        inverse * (grad_student - student * jnp.sum(student * grad_student, axis=-1, keepdims=True))
    ).astype(jnp.bfloat16)

    grad_rows = lax.dot_general(
        one_hot(row_order(core), 1152),
        grad_projected,
        (((1,), (1,)), ((), ())),
        preferred_element_type=jnp.float32,
    ).astype(jnp.bfloat16)
    grad_rows = exchange(grad_rows.reshape(4, 320, rows), FIRST)
    line_grad = lax.dot_general(
        grad_rows, features, (((0, 2), (0, 1)), ((), ())), preferred_element_type=jnp.float32
    )
    line_parts = exchange(line_grad.reshape(4, 80, 768), SECOND)
    kept, sent = column_sums(core, line_parts, other_losses)
    arrived = from_twin(sent)
    chip_grad = kept + arrived[:80]
    row_loss = (losses[0] + arrived[80, :rows]) / rows

    column_grad = jnp.pad(chip_grad.reshape(16, 15, 128), ((0, 0), (0, 1), (0, 0)))
    own_grad = jnp.sum(exchange(column_grad, COLUMN), axis=0)[:15].reshape(5, 384)

    def adam(head_grad, first, second, weights):
        new_first = beta_one * first + (1.0 - beta_one) * head_grad
        new_second = beta_two * second + (1.0 - beta_two) * head_grad * head_grad
        first_hat = new_first / (1.0 - beta_one**adam_step)
        second_hat = new_second / (1.0 - beta_two**adam_step)
        weights = weights.astype(jnp.float32)
        updated = weights - learn_rate * (
            first_hat / (jnp.sqrt(second_hat) + adam_eps) + weight_decay * weights
        )
        return updated.astype(jnp.bfloat16)

    own_weights = adam(
        own_grad,
        piece(moment_first, 0),
        piece(moment_second, 0),
        weight_rows,
    )
    packed = jnp.pad(own_weights.reshape(15, 128), ((0, 1), (0, 0)))
    chip_weights = share(packed, COLUMN)[:, :15].reshape(80, 384)
    high = rounded(own_grad)
    middle = rounded(own_grad - high)
    low = own_grad - high - middle
    spare = jnp.zeros((1, 384), jnp.float32)
    grad_parts = jnp.concatenate([high, middle, low, spare], axis=0).astype(jnp.bfloat16)
    plane = share(jnp.concatenate([chip_weights, grad_parts], axis=0), PLANE).reshape(2, 768, 384)
    half = selected(xl, plane)
    new_weights, new_first, new_second = last_outputs(
        core, half, from_twin(half), moment_first, moment_second
    )
    return (row_loss, new_first, new_second, new_weights)


def solution(mesh):
    placed = (
        P(("blk", "group"), None),
        P(("blk", "group"), None),
        P(("blk", "group"), None),
        P(),
        P(),
        P("group", None),
        P("group", None),
    )
    return jax.shard_map(
        per_device,
        mesh=mesh,
        in_specs=placed,
        out_specs=(P(("blk", "group")), P("group", None), P("group", None), P()),
        check_vma=False,
    )
```

profile of v0, /device:TPU:1, one launch (start us, length us, event | category | flops | bytes accessed | tf_op | source)
XLA Modules:
  0.0 169.8 jit_solution(29492586870419902)
XLA Ops:
  0.6 2.7 %shard_map.111 = (bf16[4,128,1920]{2,1,0:T(8,128)(2,1)}, bf16[128,1152]{1,0:T(8,128)(2,1)}) custom-call(bf16[128,1152]{1,0:T(8,128)(2,1)} %texts_ref.1, bf16[128,768]{1,0:T(8,128)(2,1)} %features_ref.1, bf16[128,1152]{1,0:T(8,128)(2,1)} %teacher_ref.1), custom_call_target="tpu_custom_call" | custom-call | flops 1179648 | bytes 2949120 | tf_op jit(solution)/shard_map/pallas_call | solution.py:128
  3.4 8.7 %collective-permute-start = (bf16[128,768]{1,0:T(8,128)(2,1)}, bf16[128,768]{1,0:T(8,128)(2,1)S(1)}, u32[]{:S(2)}, u32[]{:S(2)}) collective-permute-start(bf16[128,768]{1,0:T(8,128)(2,1)} %features_ref.1), channel_id=1, source_target_pairs={{0,32},{1,33},{2,34},{3,35},{4,36},{5,37},{6,38},{7,39},{8,40},{9,... | collective-permute-start | bytes 589832 | tf_op jit(solution)/shard_map/ppermute | solution.py:92
  12.1 2.1 %collective-permute-start.1 = (bf16[128,1152]{1,0:T(8,128)(2,1)}, bf16[128,1152]{1,0:T(8,128)(2,1)S(1)}, u32[]{:S(2)}, u32[]{:S(2)}) collective-permute-start(bf16[128,1152]{1,0:T(8,128)(2,1)} %get-tuple-element.36.refs_1_), channel_id=1, source_target_pairs={{0,32},{1,33},{2,34},{3,35},{4,36},{5,37},{6,38},{7,39},{8,40},{9,... | collective-permute-start | bytes 884744 | tf_op jit(solution)/shard_map/ppermute | solution.py:92
  14.2 4.4 %all-to-all-start = ((bf16[4,128,1920]{2,1,0:T(8,128)(2,1)}), bf16[4,128,1920]{2,1,0:T(8,128)(2,1)}, u32[]{:S(2)}, u32[]{:S(2)}) async-start(bf16[4,128,1920]{2,1,0:T(8,128)(2,1)} %get-tuple-element.32), calls=%async_computation | async-start | bytes 3932160 | tf_op jit(solution)/shard_map/all_to_all | solution.py:84
  22.6 10.8 %all-to-all-done = bf16[4,128,1920]{2,1,0:T(8,128)(2,1)} async-done(((bf16[4,128,1920]{2,1,0:T(8,128)(2,1)}), bf16[4,128,1920]{2,1,0:T(8,128)(2,1)}, u32[]{:S(2)}, u32[]{:S(2)}) %all-to-all-start) | async-done | bytes 1966112 | tf_op jit(solution)/shard_map/all_to_all | solution.py:84
  34.7 2.1 %collective-permute-start.2 = (bf16[256,1152]{1,0:T(8,128)(2,1)S(1)}, bf16[256,1152]{1,0:T(8,128)(2,1)S(1)}, u32[]{:S(2)}, u32[]{:S(2)}) collective-permute-start(bf16[256,1152]{1,0:T(8,128)(2,1)S(1)} %bitcast.27), channel_id=1, source_target_pairs={{0,128},{1,129},{2,130},{3,131},{4,132},{5,133},{6,134},{7,135},{8... | collective-permute-start | bytes 1769480 | tf_op jit(solution)/shard_map/ppermute | solution.py:426
  36.8 4.6 %collective-permute-start.4 = (bf16[256,1152]{1,0:T(8,128)(2,1)S(1)}, bf16[256,1152]{1,0:T(8,128)(2,1)S(1)}, u32[]{:S(2)}, u32[]{:S(2)}) collective-permute-start(bf16[256,1152]{1,0:T(8,128)(2,1)S(1)} %bitcast.30), channel_id=1, source_target_pairs={{0,384},{1,385},{2,386},{3,387},{4,388},{5,389},{6,390},{7,391},{8... | collective-permute-start | bytes 1769480 | tf_op jit(solution)/shard_map/ppermute | solution.py:427
  41.3 1.9 %collective-permute-start.6 = (bf16[256,1152]{1,0:T(8,128)(2,1)S(1)}, bf16[256,1152]{1,0:T(8,128)(2,1)S(1)}, u32[]{:S(2)}, u32[]{:S(2)}) collective-permute-start(bf16[256,1152]{1,0:T(8,128)(2,1)S(1)} %bitcast.31), channel_id=1, source_target_pairs={{0,128},{1,129},{2,130},{3,131},{4,132},{5,133},{6,134},{7,135},{8... | collective-permute-start | bytes 1769480 | tf_op jit(solution)/shard_map/ppermute | solution.py:428
  43.3 4.6 %collective-permute-start.7 = (bf16[256,1152]{1,0:T(8,128)(2,1)S(1)}, bf16[256,1152]{1,0:T(8,128)(2,1)S(1)}, u32[]{:S(2)}, u32[]{:S(2)}) collective-permute-start(bf16[256,1152]{1,0:T(8,128)(2,1)S(1)} %bitcast.28), channel_id=1, source_target_pairs={{0,384},{1,385},{2,386},{3,387},{4,388},{5,389},{6,390},{7,391},{8... | collective-permute-start | bytes 1769480 | tf_op jit(solution)/shard_map/ppermute | solution.py:429
  47.9 1.9 %collective-permute-start.3 = (bf16[256,1152]{1,0:T(8,128)(2,1)S(1)}, bf16[256,1152]{1,0:T(8,128)(2,1)S(1)}, u32[]{:S(2)}, u32[]{:S(2)}) collective-permute-start(bf16[256,1152]{1,0:T(8,128)(2,1)S(1)} %collective-permute-done.2.refs_5_), channel_id=1, source_target_pairs={{0,128},{1,129},{2,130},{3,131},{4,132},{5,133},{6,134},{7,135},{8... | collective-permute-start | bytes 1769480 | tf_op jit(solution)/shard_map/ppermute | solution.py:430
  49.8 4.6 %collective-permute-start.5 = (bf16[256,1152]{1,0:T(8,128)(2,1)S(1)}, bf16[256,1152]{1,0:T(8,128)(2,1)S(1)}, u32[]{:S(2)}, u32[]{:S(2)}) collective-permute-start(bf16[256,1152]{1,0:T(8,128)(2,1)S(1)} %collective-permute-done.4.refs_6_), channel_id=1, source_target_pairs={{0,384},{1,385},{2,386},{3,387},{4,388},{5,389},{6,390},{7,391},{8... | collective-permute-start | bytes 1769480 | tf_op jit(solution)/shard_map/ppermute | solution.py:431
  55.6 1.8 %shard_map.112 = (f32[256,1152]{1,0:T(8,128)S(1)}, f32[256,1]{1,0:T(8,128)S(1)}) custom-call(bf16[256,1152]{1,0:T(8,128)(2,1)S(1)} %get-tuple-element.35.refs_0_, bf16[128,1152]{1,0:T(8,128)(2,1)S(1)} %copy-done.3, bf16[128,1152]{1,0:T(8,128)(2,1)S(1)} %collective-permute-done.1.refs_2_, s32[2,128]{1,0:T(2,128)S(1)} %pad_add_fusion.refs_3_, ...), custom_call_target="tpu_custom_call" | custom-call | flops 905969664 | bytes 1179648 | tf_op jit(solution)/shard_map/pallas_call | solution.py:326
  57.4 3.3 %shard_map.113 = (f32[256,1152]{1,0:T(8,128)S(1)}, f32[256,1]{1,0:T(8,128)S(1)}) custom-call(bf16[256,1152]{1,0:T(8,128)(2,1)S(1)} %get-tuple-element.35.refs_0_, bf16[128,1152]{1,0:T(8,128)(2,1)S(1)} %copy-done.3, bf16[128,1152]{1,0:T(8,128)(2,1)S(1)} %collective-permute-done.1.refs_2_, s32[2,128]{1,0:T(2,128)S(1)} %pad_add_fusion.refs_3_, ...), custom_call_target="tpu_custom_call" | custom-call | flops 1811939328 | bytes 2359296 | tf_op jit(solution)/shard_map/pallas_call | solution.py:326
  61.2 1.8 %shard_map.114 = (f32[128,1152]{1,0:T(8,128)S(1)}, f32[128,1152]{1,0:T(8,128)S(1)}, f32[1,128]{1,0:T(1,128)S(1)}, f32[8,384]{1,0:T(8,128)S(1)}) custom-call(bf16[256,1152]{1,0:T(8,128)(2,1)S(1)} %get-tuple-element.35.refs_0_, bf16[128,1152]{1,0:T(8,128)(2,1)S(1)} %copy-done.3, bf16[128,1152]{1,0:T(8,128)(2,1)S(1)} %collective-permute-done.1.refs_2_, ...), custom_call_target="tpu_custom_call" | custom-call | flops 905969664 | bytes 1179648 | tf_op jit(solution)/shard_map/pallas_call | solution.py:326
  63.0 5.5 %collective-permute-start.8 = (f32[128,1152]{1,0:T(8,128)S(1)}, f32[128,1152]{1,0:T(8,128)S(1)}, u32[]{:S(2)}, u32[]{:S(2)}) collective-permute-start(f32[128,1152]{1,0:T(8,128)S(1)} %get-tuple-element.49), channel_id=1, source_target_pairs={{0,32},{1,33},{2,34},{3,35},{4,36},{5,37},{6,38},{7,39},{8,40},{9,... | collective-permute-start | bytes 1769480 | tf_op jit(solution)/shard_map/ppermute | solution.py:92
  71.6 10.4 %all_to_all.30 = bf16[4,320,128]{2,1,0:T(8,128)(2,1)S(1)} all-to-all(bf16[4,320,128]{2,1,0:T(8,128)(2,1)S(1)} %bitcast.34), channel_id=1, replica_groups={{0,64,16,80},{128,192,144,208},{256,320,272,336},{384,448,400,464},{1,6..., dimensions={0} | all-to-all | bytes 655360 | tf_op jit(solution)/shard_map/all_to_all | solution.py:84
  82.4 11.9 %all_to_all.31.parts_ref = f32[4,80,768]{2,1,0:T(8,128)S(1)} all-to-all(f32[4,80,768]{2,1,0:T(8,128)S(1)} %bitcast.33), channel_id=1, replica_groups={{0,128,256,384},{64,192,320,448},{16,144,272,400},{80,208,336,464},{1,1..., dimensions={0} | all-to-all | bytes 1966080 | tf_op jit(solution)/shard_map/all_to_all | solution.py:84
  94.4 4.9 %collective-permute-start.9 = (f32[88,384]{1,0:T(8,128)S(1)}, f32[88,384]{1,0:T(8,128)S(1)}, u32[]{:S(2)}, u32[]{:S(2)}) collective-permute-start(f32[88,384]{1,0:T(8,128)S(1)} %get-tuple-element.52), channel_id=1, source_target_pairs={{0,32},{1,33},{2,34},{3,35},{4,36},{5,37},{6,38},{7,39},{8,40},{9,... | collective-permute-start | bytes 405512 | tf_op jit(solution)/shard_map/ppermute | solution.py:92
  100.3 21.5 %all_to_all.32 = f32[16,16,128]{2,1,0:T(8,128)S(1)} all-to-all(f32[16,16,128]{2,1,0:T(8,128)S(1)} %pad.21), channel_id=1, replica_groups={{0,1,2,3,4,5,6,7,8,9,10,11,12,13,14,15},{32,33,34,35,36,37,38,39,40,41,..., dimensions={0} | all-to-all | bytes 262144 | tf_op jit(solution)/shard_map/all_to_all | solution.py:84
  122.0 17.9 %all_to_all.33 = bf16[16,16,128]{2,1,0:T(8,128)(2,1)S(1)} all-to-all(bf16[16,16,128]{2,1,0:T(8,128)(2,1)S(1)} %broadcast_in_dim.8), channel_id=1, replica_groups={{0,1,2,3,4,5,6,7,8,9,10,11,12,13,14,15},{32,33,34,35,36,37,38,39,40,41,..., dimensions={0} | all-to-all | bytes 131072 | tf_op jit(solution)/shard_map/all_to_all | solution.py:84
  140.3 18.7 %all_to_all.34 = bf16[16,96,384]{2,1,0:T(8,128)(2,1)S(1)} all-to-all(bf16[16,96,384]{2,1,0:T(8,128)(2,1)S(1)} %broadcast_in_dim.10), channel_id=1, replica_groups={{0,128,256,384,64,192,320,448,16,144,272,400,80,208,336,464},{1,129,257..., dimensions={0} | all-to-all | bytes 2359296 | tf_op jit(solution)/shard_map/all_to_all | solution.py:84
  160.2 5.5 %collective-permute-start.10 = (bf16[1296,384]{1,0:T(8,128)(2,1)S(1)}, bf16[1296,384]{1,0:T(8,128)(2,1)S(1)}, u32[]{:S(2)}, u32[]{:S(2)}) collective-permute-start(bf16[1296,384]{1,0:T(8,128)(2,1)S(1)} %shard_map.116.half_ref), channel_id=1, source_target_pairs={{0,32},{1,33},{2,34},{3,35},{4,36},{5,37},{6,38},{7,39},{8,40},{9,... | collective-permute-start | bytes 2985992 | tf_op jit(solution)/shard_map/ppermute | solution.py:92
  166.2 1.7 collective-permute-done.10.twin_ref
  167.9 1.9 %shard_map.117 = (bf16[1152,768]{1,0:T(8,128)(2,1)}, f32[36,768]{1,0:T(8,128)}, f32[36,768]{1,0:T(8,128)}) custom-call(s32[1]{0:T(128)} %bitcast.9.core_ref, bf16[1296,384]{1,0:T(8,128)(2,1)S(1)} %shard_map.116.half_ref, bf16[1296,384]{1,0:T(8,128)(2,1)S(1)} %collective-permute-done.10.twin_ref, f32[36,768]{1,0:T(8,128)S(1)} %copy-done.2, ...), custom_call_target="tpu_custom_call" | custom-call | bytes 6291456 | tf_op jit(solution)/shard_map/pallas_call | solution.py:249
  (63 shorter events, 13.6 us)
Async XLA Ops:
  0.6 19.8 %copy-start = (bf16[1152,768]{1,0:T(8,128)(2,1)S(1)}, bf16[1152,768]{1,0:T(8,128)(2,1)}, u32[]{:S(2)}) copy-start(bf16[1152,768]{1,0:T(8,128)(2,1)} %param.12) | copy-start | bytes 5308420
  3.4 17.2 %collective-permute-start = (bf16[128,768]{1,0:T(8,128)(2,1)}, bf16[128,768]{1,0:T(8,128)(2,1)S(1)}, u32[]{:S(2)}, u32[]{:S(2)}) collective-permute-start(bf16[128,768]{1,0:T(8,128)(2,1)} %features_ref.1), channel_id=1, source_target_pairs={{0,32},{1,33},{2,34},{3,35},{4,36},{5,37},{6,38},{7,39},{8,40},{9,... | collective-permute-start | bytes 589832 | tf_op jit(solution)/shard_map/ppermute | solution.py:92
  12.1 8.5 %copy-start.6 = (bf16[128,768]{1,0:T(8,128)(2,1)S(1)}, bf16[128,768]{1,0:T(8,128)(2,1)}, u32[]{:S(2)}) copy-start(bf16[128,768]{1,0:T(8,128)(2,1)} %features_ref.1) | copy-start | bytes 589828
  12.1 10.5 %collective-permute-start.1 = (bf16[128,1152]{1,0:T(8,128)(2,1)}, bf16[128,1152]{1,0:T(8,128)(2,1)S(1)}, u32[]{:S(2)}, u32[]{:S(2)}) collective-permute-start(bf16[128,1152]{1,0:T(8,128)(2,1)} %get-tuple-element.36.refs_1_), channel_id=1, source_target_pairs={{0,32},{1,33},{2,34},{3,35},{4,36},{5,37},{6,38},{7,39},{8,40},{9,... | collective-permute-start | bytes 884744 | tf_op jit(solution)/shard_map/ppermute | solution.py:92
  14.2 19.2 %all-to-all-start = ((bf16[4,128,1920]{2,1,0:T(8,128)(2,1)}), bf16[4,128,1920]{2,1,0:T(8,128)(2,1)}, u32[]{:S(2)}, u32[]{:S(2)}) async-start(bf16[4,128,1920]{2,1,0:T(8,128)(2,1)} %get-tuple-element.32), calls=%async_computation | async-start | bytes 3932160 | tf_op jit(solution)/shard_map/all_to_all | solution.py:84
  21.4 47.2 %copy-start.7 = (f32[256]{0:T(256)}, f32[256]{0:T(256)S(1)}, u32[]{:S(2)}) copy-start(f32[256]{0:T(256)S(1)} %add_rsqrt_fusion) | copy-start | bytes 3076
  34.7 20.9 %copy-start.3 = (bf16[128,1152]{1,0:T(8,128)(2,1)S(1)}, bf16[128,1152]{1,0:T(8,128)(2,1)}, u32[]{:S(2)}) copy-start(bf16[128,1152]{1,0:T(8,128)(2,1)} %get-tuple-element.36.refs_1_) | copy-start | bytes 884740
  34.7 13.2 %collective-permute-start.2 = (bf16[256,1152]{1,0:T(8,128)(2,1)S(1)}, bf16[256,1152]{1,0:T(8,128)(2,1)S(1)}, u32[]{:S(2)}, u32[]{:S(2)}) collective-permute-start(bf16[256,1152]{1,0:T(8,128)(2,1)S(1)} %bitcast.27), channel_id=1, source_target_pairs={{0,128},{1,129},{2,130},{3,131},{4,132},{5,133},{6,134},{7,135},{8... | collective-permute-start | bytes 1769480 | tf_op jit(solution)/shard_map/ppermute | solution.py:426
  36.8 13.0 %collective-permute-start.4 = (bf16[256,1152]{1,0:T(8,128)(2,1)S(1)}, bf16[256,1152]{1,0:T(8,128)(2,1)S(1)}, u32[]{:S(2)}, u32[]{:S(2)}) collective-permute-start(bf16[256,1152]{1,0:T(8,128)(2,1)S(1)} %bitcast.30), channel_id=1, source_target_pairs={{0,384},{1,385},{2,386},{3,387},{4,388},{5,389},{6,390},{7,391},{8... | collective-permute-start | bytes 1769480 | tf_op jit(solution)/shard_map/ppermute | solution.py:427
  41.3 16.0 %collective-permute-start.6 = (bf16[256,1152]{1,0:T(8,128)(2,1)S(1)}, bf16[256,1152]{1,0:T(8,128)(2,1)S(1)}, u32[]{:S(2)}, u32[]{:S(2)}) collective-permute-start(bf16[256,1152]{1,0:T(8,128)(2,1)S(1)} %bitcast.31), channel_id=1, source_target_pairs={{0,128},{1,129},{2,130},{3,131},{4,132},{5,133},{6,134},{7,135},{8... | collective-permute-start | bytes 1769480 | tf_op jit(solution)/shard_map/ppermute | solution.py:428
  43.3 14.1 %collective-permute-start.7 = (bf16[256,1152]{1,0:T(8,128)(2,1)S(1)}, bf16[256,1152]{1,0:T(8,128)(2,1)S(1)}, u32[]{:S(2)}, u32[]{:S(2)}) collective-permute-start(bf16[256,1152]{1,0:T(8,128)(2,1)S(1)} %bitcast.28), channel_id=1, source_target_pairs={{0,384},{1,385},{2,386},{3,387},{4,388},{5,389},{6,390},{7,391},{8... | collective-permute-start | bytes 1769480 | tf_op jit(solution)/shard_map/ppermute | solution.py:429
  47.9 12.9 %collective-permute-start.3 = (bf16[256,1152]{1,0:T(8,128)(2,1)S(1)}, bf16[256,1152]{1,0:T(8,128)(2,1)S(1)}, u32[]{:S(2)}, u32[]{:S(2)}) collective-permute-start(bf16[256,1152]{1,0:T(8,128)(2,1)S(1)} %collective-permute-done.2.refs_5_), channel_id=1, source_target_pairs={{0,128},{1,129},{2,130},{3,131},{4,132},{5,133},{6,134},{7,135},{8... | collective-permute-start | bytes 1769480 | tf_op jit(solution)/shard_map/ppermute | solution.py:430
  49.8 11.4 %collective-permute-start.5 = (bf16[256,1152]{1,0:T(8,128)(2,1)S(1)}, bf16[256,1152]{1,0:T(8,128)(2,1)S(1)}, u32[]{:S(2)}, u32[]{:S(2)}) collective-permute-start(bf16[256,1152]{1,0:T(8,128)(2,1)S(1)} %collective-permute-done.4.refs_6_), channel_id=1, source_target_pairs={{0,384},{1,385},{2,386},{3,387},{4,388},{5,389},{6,390},{7,391},{8... | collective-permute-start | bytes 1769480 | tf_op jit(solution)/shard_map/ppermute | solution.py:431
  60.7 9.4 %copy-start.5 = (f32[256,1152]{1,0:T(8,128)S(1)}, f32[256,1152]{1,0:T(8,128)}, u32[]{:S(2)}) copy-start(f32[256,1152]{1,0:T(8,128)} %get-tuple-element.59) | copy-start | bytes 3538948
  63.0 7.1 %collective-permute-start.8 = (f32[128,1152]{1,0:T(8,128)S(1)}, f32[128,1152]{1,0:T(8,128)S(1)}, u32[]{:S(2)}, u32[]{:S(2)}) collective-permute-start(f32[128,1152]{1,0:T(8,128)S(1)} %get-tuple-element.49), channel_id=1, source_target_pairs={{0,32},{1,33},{2,34},{3,35},{4,36},{5,37},{6,38},{7,39},{8,40},{9,... | collective-permute-start | bytes 1769480 | tf_op jit(solution)/shard_map/ppermute | solution.py:92
  68.6 1.8 %slice-start = ((f32[256]{0:T(256)}), f32[128]{0:T(128)S(1)}, s32[]{:S(2)}) async-start(f32[256]{0:T(256)} %copy-done.7), calls=%async_computation.6 | async-start | bytes 1024 | tf_op jit(solution)/shard_map/slice | solution.py:441
  94.3 27.5 %copy-start.1 = (f32[36,768]{1,0:T(8,128)S(1)}, f32[36,768]{1,0:T(8,128)}, u32[]{:S(2)}) copy-start(f32[36,768]{1,0:T(8,128)} %second_ref.1) | copy-start | bytes 331780
  94.3 27.5 %copy-start.2 = (f32[36,768]{1,0:T(8,128)S(1)}, f32[36,768]{1,0:T(8,128)}, u32[]{:S(2)}) copy-start(f32[36,768]{1,0:T(8,128)} %first_ref.1) | copy-start | bytes 331780
  94.4 5.9 %collective-permute-start.9 = (f32[88,384]{1,0:T(8,128)S(1)}, f32[88,384]{1,0:T(8,128)S(1)}, u32[]{:S(2)}, u32[]{:S(2)}) collective-permute-start(f32[88,384]{1,0:T(8,128)S(1)} %get-tuple-element.52), channel_id=1, source_target_pairs={{0,32},{1,33},{2,34},{3,35},{4,36},{5,37},{6,38},{7,39},{8,40},{9,... | collective-permute-start | bytes 405512 | tf_op jit(solution)/shard_map/ppermute | solution.py:92
  140.2 18.7 %copy-start.4 = (s32[2,768]{1,0:T(2,128)S(1)}, s32[2,768]{1,0:T(2,128)}, u32[]{:S(2)}) copy-start(s32[2,768]{1,0:T(2,128)} %constant.221.clone.rows_ref) | copy-start | bytes 18436
  160.2 7.7 %collective-permute-start.10 = (bf16[1296,384]{1,0:T(8,128)(2,1)S(1)}, bf16[1296,384]{1,0:T(8,128)(2,1)S(1)}, u32[]{:S(2)}, u32[]{:S(2)}) collective-permute-start(bf16[1296,384]{1,0:T(8,128)(2,1)S(1)} %shard_map.116.half_ref), channel_id=1, source_target_pairs={{0,32},{1,33},{2,34},{3,35},{4,36},{5,37},{6,38},{7,39},{8,40},{9,... | collective-permute-start | bytes 2985992 | tf_op jit(solution)/shard_map/ppermute | solution.py:92
where the time goes:
time: 171 us; the launch traced here: 170 us
  blocking collectives  80.3 us (47%)
  starting transfers between devices  50.8 us (30%)
  waiting for transfers between devices  15.4 us (9%)
  Pallas kernels  12.8 us (7%)
  local copies, waits for them, and re-layouts  4.69 us (3%)
  matrix products  2.49 us (1%)
  other arithmetic  2.17 us (1%)
    all_to_all x5, blocking collectives, exchange(): lax.all_to_all(pieces, AXES, 0, 0, axis_index_groups=groups, tiled=True)  80.3 us
    ppermute x5, starting transfers between devices, from_twin(): return lax.ppermute(shard, AXES, TWIN)  26.8 us
    all_to_all x1, waiting for transfers between devices, exchange(): lax.all_to_all(pieces, AXES, 0, 0, axis_index_groups=groups, tiled=True)  10.8 us
    pallas_call x3, Pallas kernels, pair_sums(): pl.pallas_call(functools.partial(pair_kernel, places, bool(carried), last...  6.92 us
    ppermute x1, starting transfers between devices, per_device(): after_bottom = lax.ppermute(bottom, AXES, BACK)  4.57 us
    ppermute x1, starting transfers between devices, per_device(): after_top = lax.ppermute(top, AXES, BACK)  4.57 us
    ppermute x1, starting transfers between devices, per_device(): far_bottom = lax.ppermute(after_bottom, AXES, BACK)  4.57 us
    all_to_all x1, starting transfers between devices, exchange(): lax.all_to_all(pieces, AXES, 0, 0, axis_index_groups=groups, tiled=True)  4.45 us
  transfers between devices with their start and end apart: 12, of which 5 were waited for; matrix products, arithmetic and copies ran while one was open for 3% of the time, Pallas kernels for 3%

commit v1 on v0

--- a/solution.py
+++ b/solution.py
@@ -210,17 +210,11 @@
 
 
 def last_kernel(core_ref, half_ref, twin_ref, first_ref, second_ref, *outs):
-    weights_ref, new_first_ref, new_second_ref, sems = outs
+    weights_ref, new_first_ref, new_second_ref = outs
 
     def put(left, right):
-        copies = [
-            pltpu.make_async_copy(
-                ref.at[:1152, :], weights_ref.at[:, side * 384 : side * 384 + 384], sems.at[side]
-            )
-            for side, ref in enumerate((left, right))
-        ]
-        for copy in copies:
-            copy.start()
+        weights_ref[:, :384] = left[:1152, :]
+        weights_ref[:, 384:] = right[:1152, :]
         for side, ref in enumerate((left, right)):
             columns = slice(side * 384, side * 384 + 384)
             high, middle, low = (
@@ -231,8 +225,6 @@
             new_second_ref[:, columns] = (
                 beta_two * second_ref[:, columns] + (1.0 - beta_two) * grad * grad
             )
-        for copy in copies:
-            copy.wait()
 
     @pl.when(core_ref[0] == 0)
     def _():
@@ -250,8 +242,7 @@
         last_kernel,
         out_shape=(jax.ShapeDtypeStruct((1152, 768), jnp.bfloat16), moment, moment),
         in_specs=[pl.BlockSpec(memory_space=pltpu.SMEM)] + [whole] * 4,
-        out_specs=(pl.BlockSpec(memory_space=pltpu.HBM), whole, whole),
-        scratch_shapes=[pltpu.SemaphoreType.DMA((2,))],
+        out_specs=(whole,) * 3,
         compiler_params=pltpu.CompilerParams(vmem_limit_bytes=12 << 20),
         cost_estimate=pl.CostEstimate(flops=0, bytes_accessed=6 << 20, transcendentals=0),
     )(core.reshape(1), half, twin_half, moment_first, moment_second)
@@ -425,8 +416,8 @@
     bottom = near[2:, :, :1152].reshape(2 * rows, 1152)
     before_top = lax.ppermute(top, AXES, FORTH)
     after_bottom = lax.ppermute(bottom, AXES, BACK)
+    after_top = lax.ppermute(top, AXES, BACK)
     before_bottom = lax.ppermute(bottom, AXES, FORTH)
-    after_top = lax.ppermute(top, AXES, BACK)
     far_top = lax.ppermute(before_top, AXES, FORTH)
     far_bottom = lax.ppermute(after_bottom, AXES, BACK)
     sums = pair_sums(*images, [(top, 0), (bottom, 1)])

time: 171 us -> 170 us (level)
  no operation moved by 1% of the time
where the time goes in v1:
time: 170 us; the launch traced here: 169 us
  blocking collectives  80.3 us (47%)
  starting transfers between devices  50.8 us (30%)
  waiting for transfers between devices  15.4 us (9%)
  Pallas kernels  12.3 us (7%)
  local copies, waits for them, and re-layouts  4.69 us (3%)
  matrix products  2.49 us (1%)
  other arithmetic  2.17 us (1%)
    all_to_all x5, blocking collectives, exchange(): lax.all_to_all(pieces, AXES, 0, 0, axis_index_groups=groups, tiled=True)  80.3 us
    ppermute x5, starting transfers between devices, from_twin(): return lax.ppermute(shard, AXES, TWIN)  26.8 us
    all_to_all x1, waiting for transfers between devices, exchange(): lax.all_to_all(pieces, AXES, 0, 0, axis_index_groups=groups, tiled=True)  10.8 us
    pallas_call x3, Pallas kernels, pair_sums(): pl.pallas_call(functools.partial(pair_kernel, places, bool(carried), last...  6.92 us
    ppermute x1, starting transfers between devices, per_device(): after_bottom = lax.ppermute(bottom, AXES, BACK)  4.57 us
    ppermute x1, starting transfers between devices, per_device(): after_top = lax.ppermute(top, AXES, BACK)  4.57 us
    ppermute x1, starting transfers between devices, per_device(): far_bottom = lax.ppermute(after_bottom, AXES, BACK)  4.57 us
    all_to_all x1, starting transfers between devices, exchange(): lax.all_to_all(pieces, AXES, 0, 0, axis_index_groups=groups, tiled=True)  4.45 us
  transfers between devices with their start and end apart: 12, of which 5 were waited for; matrix products, arithmetic and copies ran while one was open for 3% of the time, Pallas kernels for 3%

profile of v1, /device:TPU:1, one launch (start us, length us, event | category | flops | bytes accessed | tf_op | source)
XLA Modules:
  0.0 169.4 jit_solution(12550375366359649601)
XLA Ops:
  0.6 2.7 %shard_map.111 = (bf16[4,128,1920]{2,1,0:T(8,128)(2,1)}, bf16[128,1152]{1,0:T(8,128)(2,1)}) custom-call(bf16[128,1152]{1,0:T(8,128)(2,1)} %texts_ref.1, bf16[128,768]{1,0:T(8,128)(2,1)} %features_ref.1, bf16[128,1152]{1,0:T(8,128)(2,1)} %teacher_ref.1), custom_call_target="tpu_custom_call" | custom-call | flops 1179648 | bytes 2949120 | tf_op jit(solution)/shard_map/pallas_call | solution.py:128
  3.4 8.7 %collective-permute-start = (bf16[128,768]{1,0:T(8,128)(2,1)}, bf16[128,768]{1,0:T(8,128)(2,1)S(1)}, u32[]{:S(2)}, u32[]{:S(2)}) collective-permute-start(bf16[128,768]{1,0:T(8,128)(2,1)} %features_ref.1), channel_id=1, source_target_pairs={{0,32},{1,33},{2,34},{3,35},{4,36},{5,37},{6,38},{7,39},{8,40},{9,... | collective-permute-start | bytes 589832 | tf_op jit(solution)/shard_map/ppermute | solution.py:92
  12.1 2.1 %collective-permute-start.1 = (bf16[128,1152]{1,0:T(8,128)(2,1)}, bf16[128,1152]{1,0:T(8,128)(2,1)S(1)}, u32[]{:S(2)}, u32[]{:S(2)}) collective-permute-start(bf16[128,1152]{1,0:T(8,128)(2,1)} %get-tuple-element.36.refs_1_), channel_id=1, source_target_pairs={{0,32},{1,33},{2,34},{3,35},{4,36},{5,37},{6,38},{7,39},{8,40},{9,... | collective-permute-start | bytes 884744 | tf_op jit(solution)/shard_map/ppermute | solution.py:92
  14.2 4.4 %all-to-all-start = ((bf16[4,128,1920]{2,1,0:T(8,128)(2,1)}), bf16[4,128,1920]{2,1,0:T(8,128)(2,1)}, u32[]{:S(2)}, u32[]{:S(2)}) async-start(bf16[4,128,1920]{2,1,0:T(8,128)(2,1)} %get-tuple-element.32), calls=%async_computation | async-start | bytes 3932160 | tf_op jit(solution)/shard_map/all_to_all | solution.py:84
  22.6 10.8 %all-to-all-done = bf16[4,128,1920]{2,1,0:T(8,128)(2,1)} async-done(((bf16[4,128,1920]{2,1,0:T(8,128)(2,1)}), bf16[4,128,1920]{2,1,0:T(8,128)(2,1)}, u32[]{:S(2)}, u32[]{:S(2)}) %all-to-all-start) | async-done | bytes 1966112 | tf_op jit(solution)/shard_map/all_to_all | solution.py:84
  34.7 2.1 %collective-permute-start.2 = (bf16[256,1152]{1,0:T(8,128)(2,1)S(1)}, bf16[256,1152]{1,0:T(8,128)(2,1)S(1)}, u32[]{:S(2)}, u32[]{:S(2)}) collective-permute-start(bf16[256,1152]{1,0:T(8,128)(2,1)S(1)} %bitcast.27), channel_id=1, source_target_pairs={{0,128},{1,129},{2,130},{3,131},{4,132},{5,133},{6,134},{7,135},{8... | collective-permute-start | bytes 1769480 | tf_op jit(solution)/shard_map/ppermute | solution.py:417
  36.8 4.6 %collective-permute-start.4 = (bf16[256,1152]{1,0:T(8,128)(2,1)S(1)}, bf16[256,1152]{1,0:T(8,128)(2,1)S(1)}, u32[]{:S(2)}, u32[]{:S(2)}) collective-permute-start(bf16[256,1152]{1,0:T(8,128)(2,1)S(1)} %bitcast.30), channel_id=1, source_target_pairs={{0,384},{1,385},{2,386},{3,387},{4,388},{5,389},{6,390},{7,391},{8... | collective-permute-start | bytes 1769480 | tf_op jit(solution)/shard_map/ppermute | solution.py:418
  41.3 1.9 %collective-permute-start.6 = (bf16[256,1152]{1,0:T(8,128)(2,1)S(1)}, bf16[256,1152]{1,0:T(8,128)(2,1)S(1)}, u32[]{:S(2)}, u32[]{:S(2)}) collective-permute-start(bf16[256,1152]{1,0:T(8,128)(2,1)S(1)} %bitcast.31), channel_id=1, source_target_pairs={{0,128},{1,129},{2,130},{3,131},{4,132},{5,133},{6,134},{7,135},{8... | collective-permute-start | bytes 1769480 | tf_op jit(solution)/shard_map/ppermute | solution.py:420
  43.3 4.6 %collective-permute-start.7 = (bf16[256,1152]{1,0:T(8,128)(2,1)S(1)}, bf16[256,1152]{1,0:T(8,128)(2,1)S(1)}, u32[]{:S(2)}, u32[]{:S(2)}) collective-permute-start(bf16[256,1152]{1,0:T(8,128)(2,1)S(1)} %bitcast.28), channel_id=1, source_target_pairs={{0,384},{1,385},{2,386},{3,387},{4,388},{5,389},{6,390},{7,391},{8... | collective-permute-start | bytes 1769480 | tf_op jit(solution)/shard_map/ppermute | solution.py:419
  47.9 1.9 %collective-permute-start.3 = (bf16[256,1152]{1,0:T(8,128)(2,1)S(1)}, bf16[256,1152]{1,0:T(8,128)(2,1)S(1)}, u32[]{:S(2)}, u32[]{:S(2)}) collective-permute-start(bf16[256,1152]{1,0:T(8,128)(2,1)S(1)} %collective-permute-done.2.refs_5_), channel_id=1, source_target_pairs={{0,128},{1,129},{2,130},{3,131},{4,132},{5,133},{6,134},{7,135},{8... | collective-permute-start | bytes 1769480 | tf_op jit(solution)/shard_map/ppermute | solution.py:421
  49.8 4.6 %collective-permute-start.5 = (bf16[256,1152]{1,0:T(8,128)(2,1)S(1)}, bf16[256,1152]{1,0:T(8,128)(2,1)S(1)}, u32[]{:S(2)}, u32[]{:S(2)}) collective-permute-start(bf16[256,1152]{1,0:T(8,128)(2,1)S(1)} %collective-permute-done.4.refs_6_), channel_id=1, source_target_pairs={{0,384},{1,385},{2,386},{3,387},{4,388},{5,389},{6,390},{7,391},{8... | collective-permute-start | bytes 1769480 | tf_op jit(solution)/shard_map/ppermute | solution.py:422
  55.6 1.8 %shard_map.112 = (f32[256,1152]{1,0:T(8,128)S(1)}, f32[256,1]{1,0:T(8,128)S(1)}) custom-call(bf16[256,1152]{1,0:T(8,128)(2,1)S(1)} %get-tuple-element.35.refs_0_, bf16[128,1152]{1,0:T(8,128)(2,1)S(1)} %copy-done.3, bf16[128,1152]{1,0:T(8,128)(2,1)S(1)} %collective-permute-done.1.refs_2_, s32[2,128]{1,0:T(2,128)S(1)} %pad_add_fusion.refs_3_, ...), custom_call_target="tpu_custom_call" | custom-call | flops 905969664 | bytes 1179648 | tf_op jit(solution)/shard_map/pallas_call | solution.py:317
  57.4 3.3 %shard_map.113 = (f32[256,1152]{1,0:T(8,128)S(1)}, f32[256,1]{1,0:T(8,128)S(1)}) custom-call(bf16[256,1152]{1,0:T(8,128)(2,1)S(1)} %get-tuple-element.35.refs_0_, bf16[128,1152]{1,0:T(8,128)(2,1)S(1)} %copy-done.3, bf16[128,1152]{1,0:T(8,128)(2,1)S(1)} %collective-permute-done.1.refs_2_, s32[2,128]{1,0:T(2,128)S(1)} %pad_add_fusion.refs_3_, ...), custom_call_target="tpu_custom_call" | custom-call | flops 1811939328 | bytes 2359296 | tf_op jit(solution)/shard_map/pallas_call | solution.py:317
  61.2 1.8 %shard_map.114 = (f32[128,1152]{1,0:T(8,128)S(1)}, f32[128,1152]{1,0:T(8,128)S(1)}, f32[1,128]{1,0:T(1,128)S(1)}, f32[8,384]{1,0:T(8,128)S(1)}) custom-call(bf16[256,1152]{1,0:T(8,128)(2,1)S(1)} %get-tuple-element.35.refs_0_, bf16[128,1152]{1,0:T(8,128)(2,1)S(1)} %copy-done.3, bf16[128,1152]{1,0:T(8,128)(2,1)S(1)} %collective-permute-done.1.refs_2_, ...), custom_call_target="tpu_custom_call" | custom-call | flops 905969664 | bytes 1179648 | tf_op jit(solution)/shard_map/pallas_call | solution.py:317
  63.0 5.5 %collective-permute-start.8 = (f32[128,1152]{1,0:T(8,128)S(1)}, f32[128,1152]{1,0:T(8,128)S(1)}, u32[]{:S(2)}, u32[]{:S(2)}) collective-permute-start(f32[128,1152]{1,0:T(8,128)S(1)} %get-tuple-element.49), channel_id=1, source_target_pairs={{0,32},{1,33},{2,34},{3,35},{4,36},{5,37},{6,38},{7,39},{8,40},{9,... | collective-permute-start | bytes 1769480 | tf_op jit(solution)/shard_map/ppermute | solution.py:92
  68.6 1.5 collective-permute-done.8
  71.6 10.4 %all_to_all.30 = bf16[4,320,128]{2,1,0:T(8,128)(2,1)S(1)} all-to-all(bf16[4,320,128]{2,1,0:T(8,128)(2,1)S(1)} %bitcast.34), channel_id=1, replica_groups={{0,64,16,80},{128,192,144,208},{256,320,272,336},{384,448,400,464},{1,6..., dimensions={0} | all-to-all | bytes 655360 | tf_op jit(solution)/shard_map/all_to_all | solution.py:84
  82.4 11.9 %all_to_all.31.parts_ref = f32[4,80,768]{2,1,0:T(8,128)S(1)} all-to-all(f32[4,80,768]{2,1,0:T(8,128)S(1)} %bitcast.33), channel_id=1, replica_groups={{0,128,256,384},{64,192,320,448},{16,144,272,400},{80,208,336,464},{1,1..., dimensions={0} | all-to-all | bytes 1966080 | tf_op jit(solution)/shard_map/all_to_all | solution.py:84
  94.4 4.9 %collective-permute-start.9 = (f32[88,384]{1,0:T(8,128)S(1)}, f32[88,384]{1,0:T(8,128)S(1)}, u32[]{:S(2)}, u32[]{:S(2)}) collective-permute-start(f32[88,384]{1,0:T(8,128)S(1)} %get-tuple-element.52), channel_id=1, source_target_pairs={{0,32},{1,33},{2,34},{3,35},{4,36},{5,37},{6,38},{7,39},{8,40},{9,... | collective-permute-start | bytes 405512 | tf_op jit(solution)/shard_map/ppermute | solution.py:92
  100.3 21.5 %all_to_all.32 = f32[16,16,128]{2,1,0:T(8,128)S(1)} all-to-all(f32[16,16,128]{2,1,0:T(8,128)S(1)} %pad.21), channel_id=1, replica_groups={{0,1,2,3,4,5,6,7,8,9,10,11,12,13,14,15},{32,33,34,35,36,37,38,39,40,41,..., dimensions={0} | all-to-all | bytes 262144 | tf_op jit(solution)/shard_map/all_to_all | solution.py:84
  122.0 17.9 %all_to_all.33 = bf16[16,16,128]{2,1,0:T(8,128)(2,1)S(1)} all-to-all(bf16[16,16,128]{2,1,0:T(8,128)(2,1)S(1)} %broadcast_in_dim.8), channel_id=1, replica_groups={{0,1,2,3,4,5,6,7,8,9,10,11,12,13,14,15},{32,33,34,35,36,37,38,39,40,41,..., dimensions={0} | all-to-all | bytes 131072 | tf_op jit(solution)/shard_map/all_to_all | solution.py:84
  140.3 18.7 %all_to_all.34 = bf16[16,96,384]{2,1,0:T(8,128)(2,1)S(1)} all-to-all(bf16[16,96,384]{2,1,0:T(8,128)(2,1)S(1)} %broadcast_in_dim.10), channel_id=1, replica_groups={{0,128,256,384,64,192,320,448,16,144,272,400,80,208,336,464},{1,129,257..., dimensions={0} | all-to-all | bytes 2359296 | tf_op jit(solution)/shard_map/all_to_all | solution.py:84
  160.2 5.5 %collective-permute-start.10 = (bf16[1296,384]{1,0:T(8,128)(2,1)S(1)}, bf16[1296,384]{1,0:T(8,128)(2,1)S(1)}, u32[]{:S(2)}, u32[]{:S(2)}) collective-permute-start(bf16[1296,384]{1,0:T(8,128)(2,1)S(1)} %shard_map.116.half_ref), channel_id=1, source_target_pairs={{0,32},{1,33},{2,34},{3,35},{4,36},{5,37},{6,38},{7,39},{8,40},{9,... | collective-permute-start | bytes 2985992 | tf_op jit(solution)/shard_map/ppermute | solution.py:92
  166.2 1.7 collective-permute-done.10.twin_ref
  (63 shorter events, 13.5 us)
Async XLA Ops:
  0.6 19.8 %copy-start = (bf16[1152,768]{1,0:T(8,128)(2,1)S(1)}, bf16[1152,768]{1,0:T(8,128)(2,1)}, u32[]{:S(2)}) copy-start(bf16[1152,768]{1,0:T(8,128)(2,1)} %param.12) | copy-start | bytes 5308420
  3.4 17.2 %collective-permute-start = (bf16[128,768]{1,0:T(8,128)(2,1)}, bf16[128,768]{1,0:T(8,128)(2,1)S(1)}, u32[]{:S(2)}, u32[]{:S(2)}) collective-permute-start(bf16[128,768]{1,0:T(8,128)(2,1)} %features_ref.1), channel_id=1, source_target_pairs={{0,32},{1,33},{2,34},{3,35},{4,36},{5,37},{6,38},{7,39},{8,40},{9,... | collective-permute-start | bytes 589832 | tf_op jit(solution)/shard_map/ppermute | solution.py:92
  12.1 8.5 %copy-start.6 = (bf16[128,768]{1,0:T(8,128)(2,1)S(1)}, bf16[128,768]{1,0:T(8,128)(2,1)}, u32[]{:S(2)}) copy-start(bf16[128,768]{1,0:T(8,128)(2,1)} %features_ref.1) | copy-start | bytes 589828
  12.1 10.5 %collective-permute-start.1 = (bf16[128,1152]{1,0:T(8,128)(2,1)}, bf16[128,1152]{1,0:T(8,128)(2,1)S(1)}, u32[]{:S(2)}, u32[]{:S(2)}) collective-permute-start(bf16[128,1152]{1,0:T(8,128)(2,1)} %get-tuple-element.36.refs_1_), channel_id=1, source_target_pairs={{0,32},{1,33},{2,34},{3,35},{4,36},{5,37},{6,38},{7,39},{8,40},{9,... | collective-permute-start | bytes 884744 | tf_op jit(solution)/shard_map/ppermute | solution.py:92
  14.2 19.2 %all-to-all-start = ((bf16[4,128,1920]{2,1,0:T(8,128)(2,1)}), bf16[4,128,1920]{2,1,0:T(8,128)(2,1)}, u32[]{:S(2)}, u32[]{:S(2)}) async-start(bf16[4,128,1920]{2,1,0:T(8,128)(2,1)} %get-tuple-element.32), calls=%async_computation | async-start | bytes 3932160 | tf_op jit(solution)/shard_map/all_to_all | solution.py:84
  21.4 47.2 %copy-start.7 = (f32[256]{0:T(256)}, f32[256]{0:T(256)S(1)}, u32[]{:S(2)}) copy-start(f32[256]{0:T(256)S(1)} %add_rsqrt_fusion) | copy-start | bytes 3076
  34.7 20.9 %copy-start.3 = (bf16[128,1152]{1,0:T(8,128)(2,1)S(1)}, bf16[128,1152]{1,0:T(8,128)(2,1)}, u32[]{:S(2)}) copy-start(bf16[128,1152]{1,0:T(8,128)(2,1)} %get-tuple-element.36.refs_1_) | copy-start | bytes 884740
  34.7 13.2 %collective-permute-start.2 = (bf16[256,1152]{1,0:T(8,128)(2,1)S(1)}, bf16[256,1152]{1,0:T(8,128)(2,1)S(1)}, u32[]{:S(2)}, u32[]{:S(2)}) collective-permute-start(bf16[256,1152]{1,0:T(8,128)(2,1)S(1)} %bitcast.27), channel_id=1, source_target_pairs={{0,128},{1,129},{2,130},{3,131},{4,132},{5,133},{6,134},{7,135},{8... | collective-permute-start | bytes 1769480 | tf_op jit(solution)/shard_map/ppermute | solution.py:417
  36.8 13.0 %collective-permute-start.4 = (bf16[256,1152]{1,0:T(8,128)(2,1)S(1)}, bf16[256,1152]{1,0:T(8,128)(2,1)S(1)}, u32[]{:S(2)}, u32[]{:S(2)}) collective-permute-start(bf16[256,1152]{1,0:T(8,128)(2,1)S(1)} %bitcast.30), channel_id=1, source_target_pairs={{0,384},{1,385},{2,386},{3,387},{4,388},{5,389},{6,390},{7,391},{8... | collective-permute-start | bytes 1769480 | tf_op jit(solution)/shard_map/ppermute | solution.py:418
  41.3 16.0 %collective-permute-start.6 = (bf16[256,1152]{1,0:T(8,128)(2,1)S(1)}, bf16[256,1152]{1,0:T(8,128)(2,1)S(1)}, u32[]{:S(2)}, u32[]{:S(2)}) collective-permute-start(bf16[256,1152]{1,0:T(8,128)(2,1)S(1)} %bitcast.31), channel_id=1, source_target_pairs={{0,128},{1,129},{2,130},{3,131},{4,132},{5,133},{6,134},{7,135},{8... | collective-permute-start | bytes 1769480 | tf_op jit(solution)/shard_map/ppermute | solution.py:420
  43.3 14.1 %collective-permute-start.7 = (bf16[256,1152]{1,0:T(8,128)(2,1)S(1)}, bf16[256,1152]{1,0:T(8,128)(2,1)S(1)}, u32[]{:S(2)}, u32[]{:S(2)}) collective-permute-start(bf16[256,1152]{1,0:T(8,128)(2,1)S(1)} %bitcast.28), channel_id=1, source_target_pairs={{0,384},{1,385},{2,386},{3,387},{4,388},{5,389},{6,390},{7,391},{8... | collective-permute-start | bytes 1769480 | tf_op jit(solution)/shard_map/ppermute | solution.py:419
  47.9 12.9 %collective-permute-start.3 = (bf16[256,1152]{1,0:T(8,128)(2,1)S(1)}, bf16[256,1152]{1,0:T(8,128)(2,1)S(1)}, u32[]{:S(2)}, u32[]{:S(2)}) collective-permute-start(bf16[256,1152]{1,0:T(8,128)(2,1)S(1)} %collective-permute-done.2.refs_5_), channel_id=1, source_target_pairs={{0,128},{1,129},{2,130},{3,131},{4,132},{5,133},{6,134},{7,135},{8... | collective-permute-start | bytes 1769480 | tf_op jit(solution)/shard_map/ppermute | solution.py:421
  49.8 11.4 %collective-permute-start.5 = (bf16[256,1152]{1,0:T(8,128)(2,1)S(1)}, bf16[256,1152]{1,0:T(8,128)(2,1)S(1)}, u32[]{:S(2)}, u32[]{:S(2)}) collective-permute-start(bf16[256,1152]{1,0:T(8,128)(2,1)S(1)} %collective-permute-done.4.refs_6_), channel_id=1, source_target_pairs={{0,384},{1,385},{2,386},{3,387},{4,388},{5,389},{6,390},{7,391},{8... | collective-permute-start | bytes 1769480 | tf_op jit(solution)/shard_map/ppermute | solution.py:422
  60.7 9.4 %copy-start.5 = (f32[256,1152]{1,0:T(8,128)S(1)}, f32[256,1152]{1,0:T(8,128)}, u32[]{:S(2)}) copy-start(f32[256,1152]{1,0:T(8,128)} %get-tuple-element.59) | copy-start | bytes 3538948
  63.0 7.1 %collective-permute-start.8 = (f32[128,1152]{1,0:T(8,128)S(1)}, f32[128,1152]{1,0:T(8,128)S(1)}, u32[]{:S(2)}, u32[]{:S(2)}) collective-permute-start(f32[128,1152]{1,0:T(8,128)S(1)} %get-tuple-element.49), channel_id=1, source_target_pairs={{0,32},{1,33},{2,34},{3,35},{4,36},{5,37},{6,38},{7,39},{8,40},{9,... | collective-permute-start | bytes 1769480 | tf_op jit(solution)/shard_map/ppermute | solution.py:92
  68.6 1.8 %slice-start = ((f32[256]{0:T(256)}), f32[128]{0:T(128)S(1)}, s32[]{:S(2)}) async-start(f32[256]{0:T(256)} %copy-done.7), calls=%async_computation.6 | async-start | bytes 1024 | tf_op jit(solution)/shard_map/slice | solution.py:432
  94.3 27.5 %copy-start.1 = (f32[36,768]{1,0:T(8,128)S(1)}, f32[36,768]{1,0:T(8,128)}, u32[]{:S(2)}) copy-start(f32[36,768]{1,0:T(8,128)} %second_ref.1) | copy-start | bytes 331780
  94.3 27.5 %copy-start.2 = (f32[36,768]{1,0:T(8,128)S(1)}, f32[36,768]{1,0:T(8,128)}, u32[]{:S(2)}) copy-start(f32[36,768]{1,0:T(8,128)} %first_ref.1) | copy-start | bytes 331780
  94.4 5.9 %collective-permute-start.9 = (f32[88,384]{1,0:T(8,128)S(1)}, f32[88,384]{1,0:T(8,128)S(1)}, u32[]{:S(2)}, u32[]{:S(2)}) collective-permute-start(f32[88,384]{1,0:T(8,128)S(1)} %get-tuple-element.52), channel_id=1, source_target_pairs={{0,32},{1,33},{2,34},{3,35},{4,36},{5,37},{6,38},{7,39},{8,40},{9,... | collective-permute-start | bytes 405512 | tf_op jit(solution)/shard_map/ppermute | solution.py:92
  140.2 18.7 %copy-start.4 = (s32[2,768]{1,0:T(2,128)S(1)}, s32[2,768]{1,0:T(2,128)}, u32[]{:S(2)}) copy-start(s32[2,768]{1,0:T(2,128)} %constant.221.clone.rows_ref) | copy-start | bytes 18436
  160.2 7.7 %collective-permute-start.10 = (bf16[1296,384]{1,0:T(8,128)(2,1)S(1)}, bf16[1296,384]{1,0:T(8,128)(2,1)S(1)}, u32[]{:S(2)}, u32[]{:S(2)}) collective-permute-start(bf16[1296,384]{1,0:T(8,128)(2,1)S(1)} %shard_map.116.half_ref), channel_id=1, source_target_pairs={{0,32},{1,33},{2,34},{3,35},{4,36},{5,37},{6,38},{7,39},{8,40},{9,... | collective-permute-start | bytes 2985992 | tf_op jit(solution)/shard_map/ppermute | solution.py:92
